TPU v7x, 32 devices: a whole 2x2x4 slice. The times are simulated.
32 devices in a mesh: chi: 4 (over y, x), dl: 4 (over z), cell: 2 (over core).
Axes of the slice: x: 2, y: 2, z: 4, core: 2. Of those that a mesh axis runs over, the one named last changes fastest.
Arguments:
- left_env: bfloat16 [2, 512, 512, 36], P('cell', None, 'chi'), may hold values from -6 to 6
- up_left: bfloat16 [2, 512, 36, 512], P('cell', 'chi', None, 'dl'), may hold values from -0.109375 to 0.109375
- up_center: bfloat16 [2, 512, 36, 512], P('cell', 'chi', None, 'dl'), may hold values from -0.109375 to 0.109375
- right_env: bfloat16 [2, 512, 36, 512], P('cell', 'dl'), may hold values from -0.046875 to 0.046875
- center: bfloat16 [2, 512, 512], P('cell', None, 'dl'), may hold values from -0.25 to 0.25
- ket_tensor: bfloat16 [2, 6, 6, 6, 6, 2], P('cell'), may hold values from -0.875 to 0.875
Outputs:
- left_env_new: float32 [2, 512, 36, 512], P('cell', 'chi', None, 'dl')
- new_left: float32 [2, 512, 36, 512], P('cell', 'chi', None, 'dl')
All inputs are finite; a program needn't handle non-finite values.
Results may differ from a plain program's by a relative error of at most 0.0066.
The roundings to bfloat16 on the way count: a program that leaves them out, or rounds other values in their place, can miss the bound.
Values may be sent and summed in bfloat16 or wider, within the bound.
A program may use at most 256 MiB of HBM per device.

v0:
```python
import math
import jax
import jax.numpy as jnp
from jax import lax
from jax.sharding import PartitionSpec as P

ITERS = 5
HIGH = lax.Precision.HIGH
F32 = jnp.float32
BF16 = jnp.bfloat16


def from_behind(block, axis, distance):
    devices = range(lax.axis_size(axis))
    route = [((i - distance) % len(devices), i) for i in devices]
    return lax.ppermute(block, axis, route)


def pick(rows, cols, row_of, col_of):
    r = lax.broadcasted_iota(jnp.int32, (rows, cols), 0)
    c = lax.broadcasted_iota(jnp.int32, (rows, cols), 1)
    return (row_of(r) == col_of(c)).astype(BF16)


def double_layer(tensor, pad):
    leg = tensor.shape[0]
    two = leg * leg
    phys = tensor.shape[4]
    big = two * pad

    def outer(first):

        def code(n):
            m, s = (n // pad, n % pad)
            a = m // leg if first else m % leg
            b = s // leg if first else s % leg
            return jnp.where(s < two, a * leg + b, -1)

        return code

    def same(n):
        return n

    total = None
    ket_rows = pick(big, two, outer(True), same)
    bra_rows = pick(big, two, outer(False), same)
    for p in range(phys):
        mat = tensor[:, :, :, :, p].reshape(two, two)
        ket_small = jnp.dot(ket_rows, mat, preferred_element_type=F32).astype(BF16)
        bra_small = jnp.dot(bra_rows, mat, preferred_element_type=F32).astype(BF16)
        ket = lax.dot_general(
            ket_small, ket_rows, (((1,), (1,)), ((), ())), preferred_element_type=F32
        )
        bra = lax.dot_general(
            bra_small, bra_rows, (((1,), (1,)), ((), ())), preferred_element_type=F32
        )
        total = ket * bra if total is None else total + ket * bra
    return total.astype(BF16)


def through_site(env, stacked, layer, pad):
    two = env.shape[2]
    summed = jnp.einsum("abm,asc->bmsc", env, stacked, preferred_element_type=F32).astype(BF16)
    amount, columns = (summed.shape[0], summed.shape[3])
    flat = summed.reshape(amount, two * pad, columns)
    out = jnp.einsum("tn,btc->bnc", layer, flat, preferred_element_type=F32).astype(BF16)
    return out.reshape(amount, two, pad, columns)


def shards(left_env, up_left, up_center, right_env, center, ket_tensor):
    env_local = left_env[0]
    left_iso = up_left[0]
    left_mid = up_center[0]
    env_right = right_env[0]
    bond_mat = center[0]
    site_ket = ket_tensor[0]
    chi_all = env_local.shape[0]
    leg_width = env_local.shape[2]
    pad = -(-leg_width // 8) * 8
    widen = ((0, 0), (0, pad - leg_width), (0, 0))
    rows = left_iso.shape[0]
    col_count = left_iso.shape[2]
    mid_all = lax.all_gather(left_mid, "chi", axis=0, tiled=True)
    iso_all = lax.all_gather(left_iso, "chi", axis=0, tiled=True)
    next_iso = from_behind(left_iso, "cell", -1)
    bra_iso = lax.all_gather(next_iso, "dl", axis=2, tiled=True)
    layer = double_layer(site_ket, pad)
    mixed = jnp.einsum("abm,ax->bmx", env_local, bond_mat, preferred_element_type=F32).astype(BF16)
    bond_term = jnp.einsum("bma,amc->bc", mixed, env_right, preferred_element_type=F32)
    bond_slots = lax.dynamic_update_slice(
        jnp.zeros((chi_all, chi_all), F32), bond_term, (lax.axis_index("chi") * rows, 0)
    )
    bond_full = lax.psum(bond_slots, ("chi", "dl")).astype(BF16)
    right_cut = through_site(env_local, jnp.pad(mid_all, widen), layer, pad)
    center_term = jnp.einsum(
        "bmda,amc->bdc", right_cut[:, :, :leg_width], env_right, preferred_element_type=F32
    ).astype(BF16)
    iso_all, center_term = lax.optimization_barrier((iso_all, center_term))
    center_part = lax.psum_scatter(center_term, "dl", scatter_dimension=0, tiled=True)
    cross = lax.psum(
        jnp.einsum("bdc,bdy->cy", center_part, center_part, preferred_element_type=F32),
        ("chi", "dl"),
    )
    center_all = lax.all_gather(center_part, "dl", axis=0, tiled=True)
    left_cut = through_site(env_local, jnp.pad(iso_all, widen), layer, pad)
    env_term = jnp.einsum(
        "bmdc,bdk->kmc", left_cut[:, :, :leg_width], bra_iso, preferred_element_type=F32
    ).astype(BF16)
    env_new = lax.psum_scatter(env_term, "chi", scatter_dimension=0, tiled=True).astype(F32)
    bond_wide = bond_full.astype(F32)
    gram = jnp.dot(jnp.dot(bond_wide, cross, precision=HIGH), bond_wide.T, precision=HIGH)
    one = jnp.eye(chi_all, dtype=F32)
    norm_sum = jnp.sum(gram * one)
    factor = 0.25 * math.sqrt(chi_all) / jnp.sqrt(norm_sum)
    gram = gram * (factor * factor)
    product = None
    for sweep_index in range(ITERS):
        step = 1.5 * one - 0.5 * gram
        product = step if product is None else jnp.dot(product, step, precision=HIGH)
        if sweep_index < ITERS - 1:
            gram = jnp.dot(jnp.dot(step, gram, precision=HIGH), step, precision=HIGH)
    mine = lax.dynamic_slice_in_dim(product, lax.axis_index("dl") * col_count, col_count, 1)
    weight = lax.dot_general(bond_wide, mine, (((0,), (0,)), ((), ())), precision=HIGH)
    weight = weight * (factor * math.sqrt(chi_all * leg_width))
    new_left = jnp.einsum("bdc,cx->bdx", center_all.astype(F32), weight, precision=HIGH)
    return (env_new[None], new_left[None])


def solution(mesh):
    placed = (
        P("cell", None, "chi", None),
        P("cell", "chi", None, "dl"),
        P("cell", "chi", None, "dl"),
        P("cell", "dl", None, None),
        P("cell", None, "dl"),
        P("cell", None, None, None, None, None),
    )
    return jax.shard_map(
        shards,
        mesh=mesh,
        in_specs=placed,
        out_specs=(P("cell", "chi", None, "dl"), P("cell", "chi", None, "dl")),
        check_vma=False,
    )
```

profile of v0, /device:TPU:0, one launch (start us, length us, event | category | flops | bytes accessed | tf_op | source)
XLA Modules:
  0.0 734.8 jit_solution(9040913470576968549)
XLA Ops:
  7.2 2.4 copy.25
  9.7 0.0 all-gather.11.cloned.1.call-start
  9.7 2.4 copy.24
  12.2 0.6 slice_reduce_fusion
  12.9 0.1 reshape_squeeze.6
  13.0 7.4 %fusion.45 = f32[1440,1440]{1,0:T(8,128)} fusion(bf16[36,36]{1,0:T(8,128)(2,1)S(1)} %reshape_squeeze.6, s32[1440]{0:T(1024)S(1)} %get-tuple-element.16, s32[1440]{0:T(1024)S(1)} %get-tuple-element.19, s32[1440]{0:T(1024)S(1)} %get-tuple-element.17, s32[1440]{0:T(1024)S(1)} %get-tuple-element.18, pred[1440]{0:T(1024)(128)(4,1)S(1)} %get-tuple-element.20, ...), kind=kOutput, calls=%fused_computation.59 | convolution fusion | flops 155468160 | bytes 8322912 | tf_op jit(solution)/shard_map/dot_general | solution.py:51
  20.3 11.2 %convolution_multiply_fusion.1 = f32[1440,1440]{1,0:T(8,128)} fusion(f32[1440,1440]{1,0:T(8,128)} %fusion.45, bf16[36,36]{1,0:T(8,128)(2,1)S(1)} %reshape_squeeze.6, s32[1440]{0:T(1024)S(1)} %get-tuple-element.16, s32[1440]{0:T(1024)S(1)} %get-tuple-element.19, s32[1440]{0:T(1024)S(1)} %get-tuple-element.17, s32[1440]{0:T(1024)S(1)} %get-tuple-element.18, ...), kind=kOutput, calls=%fused_computation.10 | convolution fusion | flops 157127040 | bytes 16617312 | tf_op jit(solution)/shard_map/dot_general | solution.py:54
  31.5 0.1 reshape_squeeze.7
  31.7 7.3 fusion.46
  39.0 12.5 %fusion.6 = bf16[1440,1440,1]{1,0,2:T(8,128)(2,1)} fusion(f32[1440,1440]{1,0:T(8,128)} %convolution_multiply_fusion.1, f32[1440,1440]{1,0:T(8,128)} %fusion.46, bf16[36,36]{1,0:T(8,128)(2,1)S(1)} %reshape_squeeze.7, s32[1440]{0:T(1024)S(1)} %get-tuple-element.16, s32[1440]{0:T(1024)S(1)} %get-tuple-element.19, s32[1440]{0:T(1024)S(1)} %get-tuple-element.17, ...), kind=kOutput, calls=%fused_computation.14 | convolution fusion | flops 161274240 | bytes 20764512 | tf_op jit(solution)/shard_map/dot_general | solution.py:54
  51.5 18.5 %all-gather.13.cloned.1.call-done = bf16[1,512,36,128]{1,3,2,0:T(8,128)(2,1)} async-done(((bf16[1,128,36,128]{1,3,2,0:T(8,128)(2,1)}), bf16[1,512,36,128]{1,3,2,0:T(8,128)(2,1)}) %all-gather.13.cloned.1.call-update) | async-done | bytes 4718608 | tf_op jit(solution)/shard_map/all_gather | solution.py:83
  70.1 32.3 %convert_bitcast_fusion.1 = bf16[128,36,40,128]{0,3,1,2:T(8,128)(2,1)} fusion(bf16[512,36,128]{0,2,1:T(8,128)(2,1)} %bitcast.128, bf16[1,512,128,36]{2,1,3,0:T(8,128)(2,1)} %param.6), kind=kOutput, calls=%fused_computation.1 | convolution fusion | flops 24182784000 | bytes 56623104 | tf_op jit(solution)/shard_map/abm,asc->bmsc/dot_general | solution.py:63
  102.4 57.2 %copy.26 = bf16[128,36,40,128]{3,2,1,0:T(8,128)(2,1)} copy(bf16[128,36,40,128]{0,3,1,2:T(8,128)(2,1)} %convert_bitcast_fusion.1) | data formatting | bytes 94371840 | tf_op jit(solution)/shard_map/convert_element_type | solution.py:63
  159.5 81.9 %convolution_convert_fusion.1 = bf16[128,128,1440]{1,2,0:T(8,128)(2,1)} fusion(bf16[128,1440,128]{2,1,0:T(8,128)(2,1)} %bitcast.122, bf16[1440,1440,1]{1,0,2:T(8,128)(2,1)} %fusion.6), kind=kOutput, calls=%fused_computation.7 | convolution fusion | flops 67971317760 | bytes 98519040 | tf_op jit(solution)/shard_map/tn,btc->bnc/dot_general | solution.py:66
  241.5 28.9 %bitcast_convert_fusion.1 = bf16[128,36,512]{2,0,1:T(8,128)(2,1)} fusion(bf16[1,128,36,512]{3,1,2,0:T(8,128)(2,1)S(1)} %copy-done.4, bf16[128,36,36,128]{3,2,1,0:T(8,128)(2,1)} %bitcast.130), kind=kOutput, calls=%fused_computation.12 | convolution fusion | flops 21745631232 | bytes 51904512 | tf_op jit(solution)/shard_map/bmda,amc->bdc/dot_general | solution.py:95
  270.5 1.2 copy-done.1
  271.7 2.8 collective-permute-done
  274.5 1.0 copy-done.2
  275.6 33.1 %convert_bitcast_fusion = bf16[128,36,40,128]{0,3,1,2:T(8,128)(2,1)} fusion(bf16[512,36,128]{0,2,1:T(8,128)(2,1)} %bitcast.127, bf16[1,512,128,36]{2,1,3,0:T(8,128)(2,1)} %param.6), kind=kOutput, calls=%fused_computation | convolution fusion | flops 24182784000 | bytes 56623104 | tf_op jit(solution)/shard_map/abm,asc->bmsc/dot_general | solution.py:63
  308.7 57.2 %copy.29 = bf16[128,36,40,128]{3,2,1,0:T(8,128)(2,1)} copy(bf16[128,36,40,128]{0,3,1,2:T(8,128)(2,1)} %convert_bitcast_fusion) | data formatting | bytes 94371840 | tf_op jit(solution)/shard_map/convert_element_type | solution.py:63
  365.9 82.1 %convolution_convert_fusion = bf16[128,128,1440]{1,2,0:T(8,128)(2,1)} fusion(bf16[128,1440,128]{2,1,0:T(8,128)(2,1)} %bitcast.121, bf16[1440,1440,1]{1,0,2:T(8,128)(2,1)} %fusion.6), kind=kOutput, calls=%fused_computation.6 | convolution fusion | flops 67971317760 | bytes 98519040 | tf_op jit(solution)/shard_map/tn,btc->bnc/dot_general | solution.py:66
  448.0 3.5 convolution_bitcast_fusion.1
  451.6 33.7 %bitcast_convert_fusion = bf16[36,128,512]{2,1,0:T(8,128)(2,1)} fusion(bf16[128,36,512]{2,0,1:T(8,128)(2,1)} %all-gather.7.cloned.1.call-done, bf16[128,36,36,128]{3,2,1,0:T(8,128)(2,1)} %bitcast.129), kind=kOutput, calls=%fused_computation.11 | convolution fusion | flops 21745631232 | bytes 51904512 | tf_op jit(solution)/shard_map/bmdc,bdk->kmc/dot_general | solution.py:106
  485.2 6.7 copy.45
  492.1 0.7 all-gather.9.cloned.1.call-update
  492.8 0.1 broadcast_in_dim.17
  492.9 6.6 fusion.42
  499.5 99.8 %all-reduce.6 = bf16[512,512]{1,0:T(8,128)(2,1)S(1)} all-reduce(f32[512,512]{1,0:T(8,128)S(1)} %fusion.42), channel_id=1, replica_groups=mesh['chi'=4,'dl'=4,'cell'=2] {'chi','dl'}, use_global_device_ids=true, to_apply=%region_2.3 | all-reduce | flops 262144 | bytes 1572864 | tf_op jit(solution)/shard_map/psum | solution.py:93
  599.3 2.0 fusion.171
  601.3 1.3 select_reduce_fusion
  603.4 1.0 fusion.51
  604.4 1.1 fusion.50
  605.5 1.0 fusion.53
  606.5 1.1 fusion.49
  607.6 1.0 fusion.52
  608.6 1.0 fusion.55
  609.6 1.0 fusion.54
  610.7 1.0 fusion.47
  611.7 1.0 select_subtract_fusion
  612.7 1.0 fusion.56
  613.8 1.2 fusion.48
  615.0 1.0 fusion.170
  616.0 0.5 fusion.38
  616.6 13.8 %reduce-scatter.7.cloned.1.call-done = bf16[128,4608]{1,0:T(8,128)(2,1)} async-done(((bf16[512,4608]{1,0:T(8,128)(2,1)}), bf16[128,4608]{1,0:T(8,128)(2,1)}) %reduce-scatter.7.cloned.1.call-update) | async-done | bytes 1179664
  630.4 1.7 copy.46
  632.1 1.7 copy.33
  633.8 87.6 %all-gather.9.cloned.1.call-done = bf16[128,36,512]{2,0,1:T(8,128)(2,1)} async-done(((bf16[32,36,512]{2,0,1:T(8,128)(2,1)}), bf16[128,36,512]{2,0,1:T(8,128)(2,1)}) %all-gather.9.cloned.1.call-update) | async-done | bytes 4718608 | tf_op jit(solution)/shard_map/all_gather | solution.py:104
  721.4 6.4 convolution_bitcast_fusion
  (28 shorter events, 0.4 us)
Async XLA Ops:
  7.2 485.7 %copy-start = (bf16[1,512,128]{2,1,0:T(8,128)(2,1)S(1)}, bf16[1,512,128]{2,1,0:T(8,128)(2,1)}, u32[]{:S(2)}) copy-start(bf16[1,512,128]{2,1,0:T(8,128)(2,1)} %param.10) | copy-start | bytes 393220
  7.2 5.0 copy-start.3
  7.2 62.9 %all-gather.13.cloned.1.call-start = ((), (), s32[]{:S(2)}) async-start(), calls=%async_computation.7 | async-start | bytes 5898240 | tf_op jit(solution)/shard_map/all_gather | solution.py:83
  9.7 260.7 %all-gather.11.cloned.1.call-start = ((), (), s32[]{:S(2)}) async-start(), calls=%async_computation.6 | async-start | bytes 5898240 | tf_op jit(solution)/shard_map/all_gather | solution.py:84
  12.1 435.9 %reduce-scatter.5.cloned.1.call-start = ((), (), s32[]{:S(2)}) async-start(), calls=%async_computation.3 | async-start | bytes 5898240 | tf_op jit(solution)/shard_map/reduce_scatter | solution.py:99
  159.5 81.9 %copy-start.4 = (bf16[1,128,36,512]{3,1,2,0:T(8,128)(2,1)S(1)}, bf16[1,128,36,512]{3,1,2,0:T(8,128)(2,1)}, u32[]{:S(2)}) copy-start(bf16[1,128,36,512]{3,1,2,0:T(8,128)(2,1)} %param.9) | copy-start | bytes 14155780
  270.4 1.3 copy-start.1
  270.4 181.2 %all-gather.7.cloned.1.call-start = ((), (), s32[]{:S(2)}) async-start(), calls=%async_computation.2 | async-start | bytes 5898240 | tf_op jit(solution)/shard_map/all_gather | solution.py:86
  271.7 2.8 collective-permute-start
  274.5 1.0 copy-start.2
  275.5 323.8 %all-reduce.5.cloned.1.call-start = ((), (), s32[]{:S(2)}) async-start(), calls=%async_computation.5 | async-start | bytes 2097152 | tf_op jit(solution)/shard_map/psum | solution.py:100
  451.5 178.9 %reduce-scatter.7.cloned.1.call-start = ((), (), s32[]{:S(2)}) async-start(), calls=%async_computation.8 | async-start | bytes 5898240
  492.0 229.4 %all-gather.9.cloned.1.call-start = ((), (), s32[]{:S(2)}) async-start(), calls=%async_computation.4 | async-start | bytes 5898240 | tf_op jit(solution)/shard_map/all_gather | solution.py:104
Sparse Core Ops, SparseCore 0:
  10.4 59.6 all-gather.12
  72.5 56.9 all-gather.10
  270.5 85.2 reduce-scatter.4
  357.8 89.6 all-gather.6
  453.2 112.9 all-reduce.4
  569.0 61.2 reduce-scatter.6
  632.0 89.4 all-gather.8
where the time goes:
time: 747 us; the launch traced here: 735 us
  matrix products  363 us (49%)
  local copies, waits for them, and re-layouts  133 us (18%)
  waiting for transfers between devices  124 us (17%)
  blocking collectives  99.8 us (13%)
  between operations  15.2 us (2%)
    dot_general x2, matrix products, through_site(): jnp.einsum('tn,btc->bnc', layer, flat, preferred_element_type=F32)  164 us
    convert_element_type x2, local copies, waits for them, and re-layouts, through_site(): jnp.einsum('abm,asc->bmsc', env, stacked, preferred_element_type=F32)  114 us
    psum x1, blocking collectives, shards(): bond_full = lax.psum(bond_slots, ('chi', 'dl')).astype(BF16)  99.8 us
    all_gather x1, waiting for transfers between devices, shards(): center_all = lax.all_gather(center_part, 'dl', axis=0, tiled=True)  87.6 us
    dot_general x2, matrix products, through_site(): jnp.einsum('abm,asc->bmsc', env, stacked, preferred_element_type=F32)  65.4 us
    dot_general x1, matrix products, shards(): jnp.einsum('bmdc,bdk->kmc', left_cut[:, :, :leg_width], bra_iso, preferre...  33.7 us
    dot_general x1, matrix products, shards(): jnp.einsum('bmda,amc->bdc', right_cut[:, :, :leg_width], env_right, prefe...  28.9 us
    dot_general x2, matrix products, double_layer(): lax.dot_general(bra_small, bra_rows, (((1,), (1,)), ((), ())), preferred_...  23.8 us
  transfers between devices with their start and end apart: 8, of which 4 were waited for; matrix products, arithmetic and copies ran while one was open for 66% of the time, Pallas kernels for 0%

commit v1 on v0

--- a/solution.py
+++ b/solution.py
@@ -90,7 +90,7 @@
     bond_slots = lax.dynamic_update_slice(
         jnp.zeros((chi_all, chi_all), F32), bond_term, (lax.axis_index("chi") * rows, 0)
     )
-    bond_full = lax.psum(bond_slots, ("chi", "dl")).astype(BF16)
+    bond_full = lax.psum(lax.psum(bond_slots, "dl"), "chi").astype(BF16)
     right_cut = through_site(env_local, jnp.pad(mid_all, widen), layer, pad)
     center_term = jnp.einsum(
         "bmda,amc->bdc", right_cut[:, :, :leg_width], env_right, preferred_element_type=F32

time: 747 us -> 797 us (1.067)
  waiting for transfers between devices: 124 us -> 226 us
  blocking collectives: 99.8 us -> 46.4 us
    psum x1, waiting for transfers between devices: 0.02 us -> 73.4 us  [shards(): lax.psum(jnp.einsum('bdc,bdy->cy', center_part, center_part, preferred_el...]
    psum x1, blocking collectives: 99.8 us -> 46.4 us  [shards(): bond_full = lax.psum(lax.psum(bond_slots, 'dl'), 'chi').astype(BF16)]
    unnamed x8 -> x9, waiting for transfers between devices: 14.6 us -> 43 us
    unnamed x15 -> x19, local copies, waits for them, and re-layouts: 17.2 us -> 18.1 us
  transfers between devices with their start and end apart: 8 -> 9, of which waited for: 4 -> 5; matrix products, arithmetic and copies ran while one was open for 66% -> 62% of each run, Pallas kernels for 0% -> 0%
where the time goes in v1:
time: 797 us; the launch traced here: 785 us
  matrix products  363 us (46%)
  waiting for transfers between devices  226 us (28%)
  local copies, waits for them, and re-layouts  135 us (17%)
  blocking collectives  46.4 us (6%)
  between operations  15.3 us (2%)
    dot_general x2, matrix products, through_site(): jnp.einsum('tn,btc->bnc', layer, flat, preferred_element_type=F32)  164 us
    convert_element_type x2, local copies, waits for them, and re-layouts, through_site(): jnp.einsum('abm,asc->bmsc', env, stacked, preferred_element_type=F32)  116 us
    all_gather x1, waiting for transfers between devices, shards(): center_all = lax.all_gather(center_part, 'dl', axis=0, tiled=True)  87.6 us
    psum x1, waiting for transfers between devices, shards(): lax.psum(jnp.einsum('bdc,bdy->cy', center_part, center_part, preferred_el...  73.4 us
    dot_general x2, matrix products, through_site(): jnp.einsum('abm,asc->bmsc', env, stacked, preferred_element_type=F32)  64.6 us
    psum x1, blocking collectives, shards(): bond_full = lax.psum(lax.psum(bond_slots, 'dl'), 'chi').astype(BF16)  46.4 us
    unnamed x9, waiting for transfers between devices  43 us
    dot_general x1, matrix products, shards(): jnp.einsum('bmdc,bdk->kmc', left_cut[:, :, :leg_width], bra_iso, preferre...  33.5 us
  transfers between devices with their start and end apart: 9, of which 5 were waited for; matrix products, arithmetic and copies ran while one was open for 62% of the time, Pallas kernels for 0%

profile of v1, /device:TPU:0, one launch (start us, length us, event | category | flops | bytes accessed | tf_op | source)
XLA Modules:
  0.0 785.1 jit_solution(11760038368742615049)
XLA Ops:
  7.2 2.4 copy.25
  9.7 2.4 copy.24
  12.2 0.6 slice_reduce_fusion
  12.9 0.1 reshape_squeeze.6
  13.0 7.4 fusion.45
  20.3 11.2 %convolution_multiply_fusion.1 = f32[1440,1440]{1,0:T(8,128)} fusion(f32[1440,1440]{1,0:T(8,128)} %fusion.45, bf16[36,36]{1,0:T(8,128)(2,1)S(1)} %reshape_squeeze.6, s32[1440]{0:T(1024)S(1)} %get-tuple-element.16, s32[1440]{0:T(1024)S(1)} %get-tuple-element.19, s32[1440]{0:T(1024)S(1)} %get-tuple-element.17, s32[1440]{0:T(1024)S(1)} %get-tuple-element.18, ...), kind=kOutput, calls=%fused_computation.10 | convolution fusion | flops 157127040 | bytes 16617312 | tf_op jit(solution)/shard_map/dot_general | solution.py:54
  31.6 7.3 fusion.46
  39.0 12.6 %fusion.6 = bf16[1440,1440,1]{1,0,2:T(8,128)(2,1)} fusion(f32[1440,1440]{1,0:T(8,128)} %convolution_multiply_fusion.1, f32[1440,1440]{1,0:T(8,128)} %fusion.46, bf16[36,36]{1,0:T(8,128)(2,1)S(1)} %reshape_squeeze.7, s32[1440]{0:T(1024)S(1)} %get-tuple-element.16, s32[1440]{0:T(1024)S(1)} %get-tuple-element.19, s32[1440]{0:T(1024)S(1)} %get-tuple-element.17, ...), kind=kOutput, calls=%fused_computation.14 | convolution fusion | flops 161274240 | bytes 20764512 | tf_op jit(solution)/shard_map/dot_general | solution.py:54
  51.5 18.6 %all-gather.13.cloned.1.call-done = bf16[1,512,36,128]{1,3,2,0:T(8,128)(2,1)} async-done(((bf16[1,128,36,128]{1,3,2,0:T(8,128)(2,1)}), bf16[1,512,36,128]{1,3,2,0:T(8,128)(2,1)}) %all-gather.13.cloned.1.call-update) | async-done | bytes 4718608 | tf_op jit(solution)/shard_map/all_gather | solution.py:83
  70.1 32.3 %convert_bitcast_fusion.1 = bf16[128,36,40,128]{0,3,1,2:T(8,128)(2,1)} fusion(bf16[512,36,128]{0,2,1:T(8,128)(2,1)} %bitcast.128, bf16[1,512,128,36]{2,1,3,0:T(8,128)(2,1)} %param.6), kind=kOutput, calls=%fused_computation.1 | convolution fusion | flops 24182784000 | bytes 56623104 | tf_op jit(solution)/shard_map/abm,asc->bmsc/dot_general | solution.py:63
  102.4 57.8 %copy.26 = bf16[128,36,40,128]{3,2,1,0:T(8,128)(2,1)} copy(bf16[128,36,40,128]{0,3,1,2:T(8,128)(2,1)} %convert_bitcast_fusion.1) | data formatting | bytes 94371840 | tf_op jit(solution)/shard_map/convert_element_type | solution.py:63
  160.2 81.9 %convolution_convert_fusion.1 = bf16[128,128,1440]{1,2,0:T(8,128)(2,1)} fusion(bf16[128,1440,128]{2,1,0:T(8,128)(2,1)} %bitcast.122, bf16[1440,1440,1]{1,0,2:T(8,128)(2,1)} %fusion.6), kind=kOutput, calls=%fused_computation.7 | convolution fusion | flops 67971317760 | bytes 98519040 | tf_op jit(solution)/shard_map/tn,btc->bnc/dot_general | solution.py:66
  242.1 28.9 %bitcast_convert_fusion.1 = bf16[128,36,512]{2,0,1:T(8,128)(2,1)} fusion(bf16[1,128,36,512]{3,1,2,0:T(8,128)(2,1)S(1)} %copy-done.6, bf16[128,36,36,128]{3,2,1,0:T(8,128)(2,1)} %bitcast.130), kind=kOutput, calls=%fused_computation.12 | convolution fusion | flops 21745631232 | bytes 51904512 | tf_op jit(solution)/shard_map/bmda,amc->bdc/dot_general | solution.py:95
  271.1 1.2 copy-done.3
  272.3 2.8 collective-permute-done
  275.2 1.0 copy-done.4
  276.2 0.1 broadcast_in_dim.17
  276.4 7.3 fusion.42
  283.7 1.0 copy-done.2
  284.7 32.3 %convert_bitcast_fusion = bf16[128,36,40,128]{0,3,1,2:T(8,128)(2,1)} fusion(bf16[512,36,128]{0,2,1:T(8,128)(2,1)} %bitcast.127, bf16[1,512,128,36]{2,1,3,0:T(8,128)(2,1)} %param.6), kind=kOutput, calls=%fused_computation | convolution fusion | flops 24182784000 | bytes 56623104 | tf_op jit(solution)/shard_map/abm,asc->bmsc/dot_general | solution.py:63
  317.0 57.9 %copy.29 = bf16[128,36,40,128]{3,2,1,0:T(8,128)(2,1)} copy(bf16[128,36,40,128]{0,3,1,2:T(8,128)(2,1)} %convert_bitcast_fusion) | data formatting | bytes 94371840 | tf_op jit(solution)/shard_map/convert_element_type | solution.py:63
  375.0 81.8 %convolution_convert_fusion = bf16[128,128,1440]{1,2,0:T(8,128)(2,1)} fusion(bf16[128,1440,128]{2,1,0:T(8,128)(2,1)} %bitcast.121, bf16[1440,1440,1]{1,0,2:T(8,128)(2,1)} %fusion.6), kind=kOutput, calls=%fused_computation.6 | convolution fusion | flops 67971317760 | bytes 98519040 | tf_op jit(solution)/shard_map/tn,btc->bnc/dot_general | solution.py:66
  456.7 3.5 convolution_bitcast_fusion.1
  460.3 33.5 %bitcast_convert_fusion = bf16[36,128,512]{2,1,0:T(8,128)(2,1)} fusion(bf16[128,36,512]{2,0,1:T(8,128)(2,1)} %all-gather.7.cloned.1.call-done, bf16[128,36,36,128]{3,2,1,0:T(8,128)(2,1)} %bitcast.129), kind=kOutput, calls=%fused_computation.11 | convolution fusion | flops 21745631232 | bytes 51904512 | tf_op jit(solution)/shard_map/bmdc,bdk->kmc/dot_general | solution.py:106
  493.8 6.7 copy.45
  500.6 0.7 all-gather.9.cloned.1.call-update
  501.4 46.4 %all-reduce.9 = bf16[512,512]{1,0:T(8,128)(2,1)S(1)} all-reduce(f32[512,512]{1,0:T(8,128)} %all-reduce.6.cloned.1.call-done), channel_id=1, replica_groups=mesh['chi'=4,'dl'=4,'cell'=2] {'chi'}, use_global_device_ids=true, to_apply=%region_3.4 | all-reduce | flops 262144 | bytes 1572864 | tf_op jit(solution)/shard_map/psum | solution.py:93
  547.8 73.4 %all-reduce.8.cloned.1.call-done = f32[512,512]{1,0:T(8,128)} async-done(((f32[512,512]{1,0:T(8,128)}), f32[512,512]{1,0:T(8,128)}) %all-reduce.8.cloned.1.call-update) | async-done | bytes 1048592 | tf_op jit(solution)/shard_map/psum | solution.py:100
  621.2 2.0 fusion.171
  623.2 1.3 select_reduce_fusion
  625.2 1.0 fusion.51
  626.2 1.1 fusion.50
  627.3 1.0 fusion.53
  628.3 1.1 fusion.49
  629.4 1.0 fusion.52
  630.4 1.0 fusion.55
  631.5 1.0 fusion.54
  632.5 1.0 fusion.47
  633.5 1.0 select_subtract_fusion
  634.6 1.0 fusion.56
  635.6 1.2 fusion.48
  636.9 1.0 fusion.170
  637.9 0.5 fusion.38
  638.4 42.2 %reduce-scatter.7.cloned.1.call-done = bf16[128,4608]{1,0:T(8,128)(2,1)} async-done(((bf16[512,4608]{1,0:T(8,128)(2,1)}), bf16[128,4608]{1,0:T(8,128)(2,1)}) %reduce-scatter.7.cloned.1.call-update) | async-done | bytes 1179664
  680.6 1.7 copy.46
  682.3 1.7 copy.33
  684.1 87.6 %all-gather.9.cloned.1.call-done = bf16[128,36,512]{2,0,1:T(8,128)(2,1)} async-done(((bf16[32,36,512]{2,0,1:T(8,128)(2,1)}), bf16[128,36,512]{2,0,1:T(8,128)(2,1)}) %all-gather.9.cloned.1.call-update) | async-done | bytes 4718608 | tf_op jit(solution)/shard_map/all_gather | solution.py:104
  771.7 6.3 convolution_bitcast_fusion
  (35 shorter events, 0.7 us)
Async XLA Ops:
  7.2 269.2 %copy-start = (bf16[1,512,128]{2,1,0:T(8,128)(2,1)S(1)}, bf16[1,512,128]{2,1,0:T(8,128)(2,1)}, u32[]{:S(2)}) copy-start(bf16[1,512,128]{2,1,0:T(8,128)(2,1)} %param.10) | copy-start | bytes 393220
  7.2 5.0 copy-start.5
  7.2 62.9 %all-gather.13.cloned.1.call-start = ((), (), s32[]{:S(2)}) async-start(), calls=%async_computation.8 | async-start | bytes 5898240 | tf_op jit(solution)/shard_map/all_gather | solution.py:83
  9.7 261.4 %all-gather.11.cloned.1.call-start = ((), (), s32[]{:S(2)}) async-start(), calls=%async_computation.7 | async-start | bytes 5898240 | tf_op jit(solution)/shard_map/all_gather | solution.py:84
  12.1 444.6 %reduce-scatter.5.cloned.1.call-start = ((), (), s32[]{:S(2)}) async-start(), calls=%async_computation.3 | async-start | bytes 5898240 | tf_op jit(solution)/shard_map/reduce_scatter | solution.py:99
  160.2 81.9 %copy-start.6 = (bf16[1,128,36,512]{3,1,2,0:T(8,128)(2,1)S(1)}, bf16[1,128,36,512]{3,1,2,0:T(8,128)(2,1)}, u32[]{:S(2)}) copy-start(bf16[1,128,36,512]{3,1,2,0:T(8,128)(2,1)} %param.9) | copy-start | bytes 14155780
  271.0 1.3 copy-start.3
  271.1 189.3 %all-gather.7.cloned.1.call-start = ((), (), s32[]{:S(2)}) async-start(), calls=%async_computation.2 | async-start | bytes 5898240 | tf_op jit(solution)/shard_map/all_gather | solution.py:86
  272.3 2.8 collective-permute-start
  275.2 1.0 copy-start.4
  276.2 225.2 %all-reduce.6.cloned.1.call-start = ((), (), s32[]{:S(2)}) async-start(), calls=%async_computation.5 | async-start | bytes 2097152 | tf_op jit(solution)/shard_map/psum | solution.py:93
  283.7 1.0 copy-start.2
  284.7 336.5 %all-reduce.8.cloned.1.call-start = ((), (), s32[]{:S(2)}) async-start(), calls=%async_computation.6 | async-start | bytes 2097152 | tf_op jit(solution)/shard_map/psum | solution.py:100
  460.3 220.4 %reduce-scatter.7.cloned.1.call-start = ((), (), s32[]{:S(2)}) async-start(), calls=%async_computation.9 | async-start | bytes 5898240
  500.6 271.1 %all-gather.9.cloned.1.call-start = ((), (), s32[]{:S(2)}) async-start(), calls=%async_computation.4 | async-start | bytes 5898240 | tf_op jit(solution)/shard_map/all_gather | solution.py:104
  682.3 95.7 %copy-start.1 = (bf16[1,512,128]{2,1,0:T(8,128)(2,1)S(1)}, bf16[1,512,128]{2,1,0:T(8,128)(2,1)}, u32[]{:S(2)}) copy-start(bf16[1,512,128]{2,1,0:T(8,128)(2,1)} %param.10) | copy-start | bytes 393220
Sparse Core Ops, SparseCore 0:
  10.4 59.6 all-gather.12
  72.5 56.9 all-gather.10
  271.2 85.2 reduce-scatter.4
  358.4 89.6 all-gather.6
  450.9 50.0 all-reduce.5
  506.9 114.1 all-reduce.7
  624.4 56.1 reduce-scatter.6
  682.3 89.3 all-gather.8
